TPU v7x, 32 devices: a whole 2x2x4 slice. The times are simulated.
32 devices in a mesh: row: 4 (over y, x), col: 8 (over z, core).
Axes of the slice: x: 2, y: 2, z: 4, core: 2. Of those that a mesh axis runs over, the one named last changes fastest.
Arguments:
- node_features: bfloat16 [4096, 1024], P(('row', 'col')), may hold values from -6 to 6
- norm_gain: float32 [1024], replicated, may hold values from 0.5 to 1.5
- w_query: bfloat16 [1024, 1024], replicated, may hold values from -0.1875 to 0.1875
- w_keyvalue: bfloat16 [1024, 2048], replicated, may hold values from -0.1875 to 0.1875
- w_out: bfloat16 [1024, 1024], replicated, may hold values from -0.1875 to 0.1875
- bias_table: float32 [32, 8], replicated, may hold values from -4 to 4
- edge_slope: float32 [8], replicated, may hold values from 0.5 to 1.5
- pair_blocks: int32 [4, 8, 2, 16], P('row', 'col'), may hold values from -1 to 7, as said below
- bucket_ids: int32 [4, 8, 16, 128, 128], P('row', 'col'), may hold values from 0 to 31
- edge_weight: bfloat16 [4, 8, 4, 4, 128, 128], P('row', 'col'), may hold values from -4 to 240
Outputs:
- node_out: bfloat16 [4096, 1024], P(('row', 'col'))
Inputs may be any that keep to these rules, and one draw needn't show every extreme that they name: `pair_blocks`: slots of a tile with query block -1 are empty and name key block 0. The listed pairs of a tile are distinct; each tile (r, c) lists, among the slots from t = r, every block of node shard r * 8 + c paired with itself. Up to 4 slots from one owner to one row range are used, and some tile uses all 16 of its slots.
All inputs are finite; a program needn't handle non-finite values.
Results may differ from a plain program's by a relative error of at most 0.005.
Values may be sent and summed in bfloat16 or wider, within the bound.
A program may use at most 256 MiB of HBM per device.

v0:
```python
import functools

import jax
import jax.numpy as jnp
from jax import lax
from jax.experimental import pallas as pl
from jax.experimental.pallas import tpu as pltpu
from jax.sharding import PartitionSpec as P

EPSILON = 1e-05
LOW_FLOOR = -1e30
CORES = 2
MESH = pl.DeviceIdType.MESH
LANES = 128
ROOM = 6 * 2**20


def normalize(features, gain_vec):
    as_float = features.astype(jnp.float32)
    centered = as_float - jnp.mean(as_float, axis=-1, keepdims=True)
    variance = jnp.mean(centered * centered, axis=-1, keepdims=True)
    return (centered * lax.rsqrt(variance + EPSILON) * gain_vec).astype(jnp.bfloat16)


def greet(partners):
    barrier = pltpu.get_barrier_semaphore()
    for partner in partners:
        pl.semaphore_signal(barrier, inc=1, device_id=partner, device_id_type=MESH)
    pl.semaphore_wait(barrier, len(partners))


def exchange(
    n_row, n_chip, x_in, gain_in, e_in, wq_in, w_in, q_out, k_out, v_out, e_out,
    q_in, n_in, n_buf, wq_buf, w_buf, send_sem, recv_sem, chip_sem, line_sem, own_sem,
):
    row, col = lax.axis_index("row"), lax.axis_index("col")
    chip, core = col // CORES, col % CORES
    sibling = (row, chip * CORES + (1 - core))
    chips = [(row, ((chip + k) % n_chip) * CORES + core) for k in range(1, n_chip)]
    rows = [((row + k) % n_row, col) for k in range(1, n_row)]
    width = n_in.shape[1]
    query_weights = pltpu.make_async_copy(wq_in, wq_buf, own_sem.at[3])
    weights = pltpu.make_async_copy(w_in, w_buf, own_sem.at[2])
    query_weights.start()
    greet(chips + [sibling] + rows)

    def remote(src, dst, send, recv, where):
        return pltpu.make_async_remote_copy(
            src_ref=src,
            dst_ref=dst,
            send_sem=send,
            recv_sem=recv,
            device_id=where,
            device_id_type=MESH,
        )

    def hop(step, way):
        origin = chip - way * step
        spot = origin * CORES + core
        copy = remote(
            q_in if step == 0 else q_out.at[spot],
            q_out.at[spot],
            line_sem.at[step, (way + 1) // 2],
            chip_sem.at[origin],
            (row, (chip + way) * CORES + core),
        )
        onward = (chip + way >= 0) & (chip + way < n_chip)
        return copy, onward, (origin >= 0) & (origin < n_chip), spot, origin

    weights.start()
    e_send = [
        remote(
            e_in.at[where[0]], e_out.at[row], send_sem.at[n_row + k], recv_sem.at[n_row + k], where
        )
        for k, where in enumerate(rows, 1)
    ]
    n_in[...] = normalize(x_in[...], gain_in[...])
    query_weights.wait()
    n_send = [
        remote(n_in, n_buf.at[k], send_sem.at[k], recv_sem.at[k], where)
        for k, where in enumerate(rows, 1)
    ]
    chunk = 2 * LANES

    @pl.loop(0, width // chunk)
    def _(step):
        left = pl.multiple_of(step * chunk, chunk)
        q_in[:, pl.ds(left, chunk)] = jnp.dot(
            n_in[...], wq_buf[:, pl.ds(left, chunk)], preferred_element_type=jnp.float32
        ).astype(q_in.dtype)

    for copy in n_send:
        copy.start()
    for way in (1, -1):
        copy, onward, _, _, _ = hop(0, way)

        @pl.when(onward)
        def _():
            copy.start()

    for copy in e_send:
        copy.start()
    pair_send = remote(q_in, q_out.at[col], send_sem.at[0], recv_sem.at[0], sibling)
    pair_send.start()
    own = [
        pltpu.make_async_copy(q_in, q_out.at[col], own_sem.at[0]),
        pltpu.make_async_copy(e_in.at[row], e_out.at[row], own_sem.at[1]),
    ]
    for copy in own:
        copy.start()

    def project(rows_ref, spot):
        hidden = rows_ref[...]

        @pl.loop(0, width // chunk)
        def _(step):
            left = pl.multiple_of(step * chunk, chunk)
            k_out[spot, :, pl.ds(left, chunk)] = jnp.dot(
                hidden, w_buf[:, pl.ds(left, chunk)], preferred_element_type=jnp.float32
            ).astype(k_out.dtype)
            right = pl.multiple_of(width + left, chunk)
            value = jnp.dot(hidden, w_buf[:, pl.ds(right, chunk)], preferred_element_type=jnp.float32)
            v_out[spot, pl.ds(left, chunk), :] = value.T.astype(v_out.dtype)

    weights.wait()
    project(n_in, row)

    def pass_on(step):
        for way in (1, -1):
            copy, onward, real, spot, origin = hop(step, way)

            @pl.when(real)
            def _():
                arrived = q_out.at[spot]
                copy.wait_recv()
                remote(
                    arrived,
                    arrived,
                    send_sem.at[2 * n_row + origin],
                    recv_sem.at[2 * n_row + origin],
                    sibling,
                ).start()

            if step < n_chip - 1:

                @pl.when(real & onward)
                def _():
                    hop(step, way)[0].start()

    for k in range(1, max(n_row, n_chip)):
        if k < n_chip:
            pass_on(k)
        if k < n_row:
            n_send[k - 1].wait_recv()
            project(n_buf.at[k], (row + n_row - k) % n_row)

    for way in (1, -1):
        for step in range(n_chip - 1):
            copy, onward, real, _, _ = hop(step, way)

            @pl.when(real & onward)
            def _():
                copy.wait_send()

        for step in range(1, n_chip):
            _, _, real, spot, origin = hop(step, way)

            @pl.when(real)
            def _():
                remote(
                    q_out.at[spot],
                    q_out.at[spot],
                    send_sem.at[2 * n_row + origin],
                    recv_sem.at[2 * n_row + origin],
                    sibling,
                ).wait()

    for copy in n_send:
        copy.wait_send()
    for copy in e_send + [pair_send]:
        copy.wait()
    for copy in own:
        copy.wait()


def attend(
    slot_cap, scale, pairs, slope, bias_ref, q_ref, k_ref, v_ref, e_ref, b_ref, o_ref, l_ref,
    m_acc, s_acc, o_acc, table, scores,
):
    query_count, heads, tile = l_ref.shape
    dim = q_ref.shape[2] // heads
    buckets_in = bias_ref.shape[1]
    m_acc[...] = jnp.full(m_acc.shape, LOW_FLOOR, jnp.float32)
    s_acc[...] = jnp.zeros(s_acc.shape, jnp.float32)
    o_acc[...] = jnp.zeros(o_acc.shape, jnp.float32)
    table[...] = jnp.zeros(table.shape, jnp.float32)
    table[:, :buckets_in] = bias_ref[...]

    def slot_step(slot, carry):
        query = pairs[0, slot]

        @pl.when(query >= 0)
        def _():
            key = pairs[1, slot] + slot // slot_cap
            buckets = b_ref[slot].T
            edges = e_ref[slot].astype(jnp.float32).T
            tops = []
            for h in range(heads):
                cols = slice(h * dim, (h + 1) * dim)
                score = lax.dot_general(
                    k_ref[key, :, cols],
                    q_ref[query, :, cols],
                    (((1,), (1,)), ((), ())),
                    preferred_element_type=jnp.float32,
                )
                entries = jnp.broadcast_to(table[h : h + 1, :], (tile, tile))
                bias = jnp.take_along_axis(entries, buckets, axis=1, mode="promise_in_bounds")
                score = score * scale + bias + slope[h] * edges
                scores[h] = score
                tops.append(jnp.max(score, axis=0, keepdims=True))
            old_max = m_acc[query]
            new_max = jnp.maximum(old_max, jnp.concatenate(tops, axis=0))
            keep = jnp.exp(old_max - new_max)
            m_acc[query] = new_max
            sums = []
            for h in range(heads):
                probs = jnp.exp(scores[h] - new_max[h : h + 1]).astype(jnp.bfloat16)
                sums.append(jnp.sum(probs.astype(jnp.float32), axis=0, keepdims=True))
                scores[h] = jnp.dot(
                    v_ref[key, h * dim : (h + 1) * dim, :], probs, preferred_element_type=jnp.float32
                )
            s_acc[query] = s_acc[query] * keep + jnp.concatenate(sums, axis=0)
            for h in range(heads):
                o_acc[query, h] = o_acc[query, h] * keep[h : h + 1] + scores[h]

        return carry

    lax.fori_loop(0, pairs.shape[1], slot_step, 0)

    def finish(query, carry):
        total = s_acc[query]
        live = total > 0.0
        safe = jnp.where(live, total, 1.0)
        l_ref[query] = jnp.where(live, m_acc[query] + jnp.log(safe), LOW_FLOOR)
        share = 1.0 / safe
        for h in range(heads):
            o_ref[query, h * dim : (h + 1) * dim, :] = (o_acc[query, h] * share[h : h + 1]).astype(
                o_ref.dtype
            )
        return carry

    lax.fori_loop(0, query_count, finish, 0)


def blend(levels, parts, heads):
    top = functools.reduce(jnp.maximum, levels)
    shares = [jnp.exp(level - top) for level in levels]
    total = functools.reduce(jnp.add, shares)
    weights = [share / total for share in shares]
    dim = parts[0].shape[0] // heads
    out = []
    for h in range(heads):
        rows = slice(h * dim, (h + 1) * dim)
        terms = [w[h : h + 1] * part[rows].astype(jnp.float32) for w, part in zip(weights, parts)]
        out.append(functools.reduce(jnp.add, terms))
    return out, top + jnp.log(total)


def partner(chip, k, n_chip):
    if n_chip & (n_chip - 1):
        return (chip + k) % n_chip
    bits = [1 << b for b in range(n_chip.bit_length() - 1)]
    return sum(((chip // bit + k // bit) % 2) * bit for bit in bits)


def combine(
    n_chip, o_ref, l_ref, a_ref, sib_o, sib_l, mix_o, mix_l, got_o, got_l, send_sem, recv_sem
):
    row, col = lax.axis_index("row"), lax.axis_index("col")
    chip, core = col // CORES, col % CORES
    heads = l_ref.shape[1]
    dim = o_ref.shape[1] // heads
    sibling = (row, chip * CORES + (1 - core))
    chips = [(row, partner(chip, k, n_chip) * CORES + core) for k in range(1, n_chip)]
    greet(chips + [sibling])

    def send(spot, src, dst, where):
        copy = pltpu.make_async_remote_copy(
            src_ref=src,
            dst_ref=dst,
            send_sem=send_sem.at[spot],
            recv_sem=recv_sem.at[spot],
            device_id=where,
            device_id_type=MESH,
        )
        copy.start()
        return copy

    half = n_chip // 2
    far = list(range(half, n_chip)) + list(range(1, half))
    order = far + [0]
    to_sibling = {}
    for k in order:
        theirs = partner(chip, k, n_chip) * CORES + (1 - core)
        to_sibling[k] = [
            send(4 * k, l_ref.at[theirs], sib_l.at[k], sibling),
            send(4 * k + 1, o_ref.at[theirs], sib_o.at[k], sibling),
        ]
    over = []

    def push(k):
        over.append(send(4 * k + 2, mix_l.at[k], got_l.at[k], chips[k - 1]))
        over.append(send(4 * k + 3, mix_o.at[k], got_o.at[k], chips[k - 1]))

    for k in far:
        for copy in to_sibling[k]:
            copy.wait_recv()
        mine = partner(chip, k, n_chip) * CORES + core
        out, level = blend([l_ref[mine], sib_l[k]], [o_ref[mine], sib_o[k]], heads)
        for h in range(heads):
            mix_o[k, h * dim : (h + 1) * dim, :] = out[h].astype(mix_o.dtype)
        mix_l[k] = level
        push(k)
    for copy in to_sibling[0]:
        copy.wait_recv()
    for copy in over:
        copy.wait_recv()
    levels = [l_ref[col], sib_l[0]] + [got_l[k] for k in range(1, n_chip)]
    parts = [o_ref[col], sib_o[0]] + [got_o[k] for k in range(1, n_chip)]
    out, _ = blend(levels, parts, heads)
    for h in range(heads):
        a_ref[h * dim : (h + 1) * dim, :] = out[h].astype(a_ref.dtype)
    for copies in to_sibling.values():
        for copy in copies:
            copy.wait_send()
    for copy in over:
        copy.wait_send()


def local(
    n_row,
    n_col,
    node_features,
    norm_gain,
    w_query,
    w_keyvalue,
    w_out,
    bias_table,
    edge_slope,
    pair_blocks,
    bucket_ids,
    edge_weight,
):
    tile, width = node_features.shape
    heads = edge_slope.shape[0]
    dim = width // heads
    n_chip = n_col // CORES
    slot_cap = edge_weight.shape[3]
    slots = n_row * slot_cap
    bf16, f32 = jnp.bfloat16, jnp.float32
    vmem = pl.BlockSpec(memory_space=pltpu.VMEM)
    smem = pl.BlockSpec(memory_space=pltpu.SMEM)
    hbm = pl.BlockSpec(memory_space=pl.ANY)

    block = 2 * tile * width
    weight_bytes = 2 * (w_query.size + w_keyvalue.size)
    exchange_bytes = (3 * n_row + 4) * block + weight_bytes + 2 * edge_weight.size
    attend_bytes = (4 * n_col + 2 * n_row) * block + 6 * slots * tile * tile
    combine_bytes = (n_col + 3 * n_chip + 2) * block
    copies = 2 * n_row + n_chip
    query_range, keys, values, edge_values = pl.pallas_call(
        functools.partial(exchange, n_row, n_chip),
        out_shape=(
            jax.ShapeDtypeStruct((n_col, tile, width), bf16),
            jax.ShapeDtypeStruct((n_row, tile, width), bf16),
            jax.ShapeDtypeStruct((n_row, width, tile), bf16),
            jax.ShapeDtypeStruct((n_row,) + edge_weight.shape[3:], edge_weight.dtype),
        ),
        in_specs=[vmem] * 3 + [hbm] * 2,
        out_specs=(hbm, vmem, vmem, hbm),
        scratch_shapes=[
            pltpu.VMEM((tile, width), bf16),
            pltpu.VMEM((tile, width), bf16),
            pltpu.VMEM((n_row, tile, width), bf16),
            pltpu.VMEM(w_query.shape, bf16),
            pltpu.VMEM(w_keyvalue.shape, bf16),
            pltpu.SemaphoreType.DMA((copies,)),
            pltpu.SemaphoreType.DMA((copies,)),
            pltpu.SemaphoreType.DMA((n_chip,)),
            pltpu.SemaphoreType.DMA((n_chip, 2)),
            pltpu.SemaphoreType.DMA((4,)),
        ],
        compiler_params=pltpu.CompilerParams(
            collective_id=0, has_side_effects=True, vmem_limit_bytes=exchange_bytes + ROOM
        ),
        name="exchange",
    )(node_features, norm_gain[None], edge_weight[0, 0], w_query, w_keyvalue)
    partial_out, partial_level = pl.pallas_call(
        functools.partial(attend, slot_cap, dim ** (-0.5)),
        out_shape=(
            jax.ShapeDtypeStruct((n_col, width, tile), bf16),
            jax.ShapeDtypeStruct((n_col, heads, tile), f32),
        ),
        in_specs=[smem, smem] + [vmem] * 6,
        out_specs=(vmem, vmem),
        scratch_shapes=[
            pltpu.VMEM((n_col, heads, tile), f32),
            pltpu.VMEM((n_col, heads, tile), f32),
            pltpu.VMEM((n_col, heads, dim, tile), f32),
            pltpu.VMEM((heads, tile), f32),
            pltpu.VMEM((heads, tile, tile), f32),
        ],
        compiler_params=pltpu.CompilerParams(vmem_limit_bytes=attend_bytes + ROOM),
        name="attend",
    )(
        pair_blocks.reshape(2, slots),
        edge_slope,
        bias_table.T,
        query_range,
        keys,
        values,
        edge_values.reshape(slots, tile, tile),
        bucket_ids.reshape(slots, tile, tile),
    )
    attention = pl.pallas_call(
        functools.partial(combine, n_chip),
        out_shape=jax.ShapeDtypeStruct((width, tile), bf16),
        in_specs=[vmem] * 2,
        out_specs=vmem,
        scratch_shapes=[
            pltpu.VMEM((n_chip, width, tile), bf16),
            pltpu.VMEM((n_chip, heads, tile), f32),
        ]
        * 3
        + [pltpu.SemaphoreType.DMA((4 * n_chip,))] * 2,
        compiler_params=pltpu.CompilerParams(
            collective_id=1, has_side_effects=True, vmem_limit_bytes=combine_bytes + ROOM
        ),
        name="combine",
    )(partial_out, partial_level)
    update = lax.dot_general(
        attention, w_out, (((0,), (0,)), ((), ())), preferred_element_type=f32
    )
    return (node_features.astype(f32) + update).astype(bf16)


def solution(mesh):
    return jax.shard_map(
        functools.partial(local, mesh.shape["row"], mesh.shape["col"]),
        mesh=mesh,
        in_specs=(
            P(("row", "col"), None),
            P(),
            P(),
            P(),
            P(),
            P(),
            P(),
            P("row", "col", None, None),
            P("row", "col", None, None, None),
            P("row", "col", None, None, None, None),
        ),
        out_specs=P(("row", "col"), None),
        check_vma=False,
    )
```

profile of v0, /device:TPU:11, one launch (start us, length us, event | category | flops | bytes accessed | tf_op | source)
XLA Modules:
  0.0 75.3 jit_solution(9749129611511389745)
XLA Ops:
  0.0 0.0 copy-start
  0.0 0.0 copy-start.1
  0.0 2.3 %copy-done.1 = bf16[1024,2048]{1,0:T(8,128)(2,1)S(1)} copy-done((bf16[1024,2048]{1,0:T(8,128)(2,1)S(1)}, bf16[1024,2048]{1,0:T(8,128)(2,1)}, u32[]{:S(2)}) %copy-start.1) | copy-done | bytes 4194328
  2.3 0.0 copy-start.2
  2.3 1.6 %copy-done.2 = bf16[1024,1024]{1,0:T(8,128)(2,1)S(1)} copy-done((bf16[1024,1024]{1,0:T(8,128)(2,1)S(1)}, bf16[1024,1024]{1,0:T(8,128)(2,1)}, u32[]{:S(2)}) %copy-start.2) | copy-done | bytes 2097176
  3.9 0.0 copy-start.4
  3.9 0.9 %copy-done.4 = bf16[128,1024]{1,0:T(8,128)(2,1)S(1)} copy-done((bf16[128,1024]{1,0:T(8,128)(2,1)S(1)}, bf16[128,1024]{1,0:T(8,128)(2,1)}, u32[]{:S(2)}) %copy-start.4) | copy-done | bytes 262168
  4.9 0.0 copy-start.6
  4.9 1.0 %copy-done.6 = bf16[1,1,4,4,128,128]{5,4,3,2,1,0:T(8,128)(2,1)S(1)} copy-done((bf16[1,1,4,4,128,128]{5,4,3,2,1,0:T(8,128)(2,1)S(1)}, bf16[1,1,4,4,128,128]{5,4,3,2,1,0:T(8,128)(2,1)}, u32[]{:S(2)}) %copy-start.6) | copy-done | bytes 524312
  5.9 0.0 copy-start.7
  5.9 0.7 copy-done.7
  6.6 0.0 copy-start.3
  6.6 0.0 copy-start.8
  6.6 0.0 copy-start.9
  6.6 0.0 copy-start.10
  6.6 22.6 %exchange.1 = (bf16[8,128,1024]{2,1,0:T(8,128)(2,1)S(1)}, bf16[4,128,1024]{2,1,0:T(8,128)(2,1)S(1)}, bf16[4,1024,128]{2,1,0:T(8,128)(2,1)S(1)}, bf16[4,4,128,128]{3,2,1,0:T(8,128)(2,1)S(1)}) custom-call(bf16[128,1024]{1,0:T(8,128)(2,1)S(1)} %copy-done.4, f32[1,1024]{1,0:T(1,128)S(1)} %bitcast.11, bf16[4,4,128,128]{3,2,1,0:T(8,128)(2,1)S(1)} %bitcast.9, ...), custom_call_target="tpu_custom_call" | custom-call | tf_op jit(solution)/shard_map/exchange/pallas_call | solution.py:371
  29.3 0.0 copy-done.3
  29.3 0.0 copy-done.8
  29.3 0.0 copy-done.9
  29.3 0.0 copy-done.10
  29.3 6.1 %attend.1 = (bf16[8,1024,128]{2,1,0:T(8,128)(2,1)S(1)}, f32[8,8,128]{2,1,0:T(8,128)S(1)}) custom-call(s32[2,16]{1,0:T(2,128)S(1)} %bitcast.13, f32[8]{0:T(128)S(1)} %copy-done.10, f32[8,32]{1,0:T(8,128)S(1)} %bitcast.12, bf16[8,128,1024]{2,1,0:T(8,128)(2,1)S(1)} %get-tuple-element.11.q_ref, bf16[4,128,1024]{2,1,0:T(8,128)(2,1)S(1)} %get-tuple-element.12.k_ref, ...), custom_call_target="tpu_custom_call" | custom-call | tf_op jit(solution)/shard_map/attend/pallas_call | solution.py:398
  35.4 0.0 copy-start.5
  35.5 38.6 %combine.1 = bf16[1024,128]{1,0:T(8,128)(2,1)S(1)} custom-call(bf16[8,1024,128]{2,1,0:T(8,128)(2,1)S(1)} %get-tuple-element.15.o_ref, f32[8,8,128]{2,1,0:T(8,128)S(1)} %get-tuple-element.16.l_ref), custom_call_target="tpu_custom_call" | custom-call | tf_op jit(solution)/shard_map/combine/pallas_call | solution.py:425
  74.1 0.0 copy-done
  74.1 0.0 copy-done.5
  74.1 1.2 %fusion = bf16[128,1024]{1,0:T(8,128)(2,1)} fusion(bf16[1024,128]{1,0:T(8,128)(2,1)S(1)} %combine.1, bf16[1024,1024]{1,0:T(8,128)(2,1)S(1)} %copy-done, bf16[128,1024]{1,0:T(8,128)(2,1)S(1)} %copy-done.5), kind=kOutput, calls=%fused_computation.1 | convolution fusion | flops 268828672 | bytes 2883584 | tf_op jit(solution)/shard_map/dot_general | solution.py:441
Async XLA Ops:
  0.0 74.1 %copy-start = (bf16[1024,1024]{1,0:T(8,128)(2,1)S(1)}, bf16[1024,1024]{1,0:T(8,128)(2,1)}, u32[]{:S(2)}) copy-start(bf16[1024,1024]{1,0:T(8,128)(2,1)} %param.14) | copy-start | bytes 6291460
  0.0 2.3 %copy-start.1 = (bf16[1024,2048]{1,0:T(8,128)(2,1)S(1)}, bf16[1024,2048]{1,0:T(8,128)(2,1)}, u32[]{:S(2)}) copy-start(bf16[1024,2048]{1,0:T(8,128)(2,1)} %w_in.1) | copy-start | bytes 12582916
  2.3 1.6 %copy-start.2 = (bf16[1024,1024]{1,0:T(8,128)(2,1)S(1)}, bf16[1024,1024]{1,0:T(8,128)(2,1)}, u32[]{:S(2)}) copy-start(bf16[1024,1024]{1,0:T(8,128)(2,1)} %wq_in.1) | copy-start | bytes 6291460
  3.9 0.9 %copy-start.4 = (bf16[128,1024]{1,0:T(8,128)(2,1)S(1)}, bf16[128,1024]{1,0:T(8,128)(2,1)}, u32[]{:S(2)}) copy-start(bf16[128,1024]{1,0:T(8,128)(2,1)} %x_in.1) | copy-start | bytes 786436
  4.9 1.0 %copy-start.6 = (bf16[1,1,4,4,128,128]{5,4,3,2,1,0:T(8,128)(2,1)S(1)}, bf16[1,1,4,4,128,128]{5,4,3,2,1,0:T(8,128)(2,1)}, u32[]{:S(2)}) copy-start(bf16[1,1,4,4,128,128]{5,4,3,2,1,0:T(8,128)(2,1)} %param.19) | copy-start | bytes 1572868
  5.9 0.7 copy-start.7
  6.6 22.7 %copy-start.3 = (s32[1,1,16,128,128]{4,3,2,1,0:T(8,128)S(1)}, s32[1,1,16,128,128]{4,3,2,1,0:T(8,128)}, u32[]{:S(2)}) copy-start(s32[1,1,16,128,128]{4,3,2,1,0:T(8,128)} %param.18) | copy-start | bytes 3145732
  6.6 22.7 %copy-start.8 = (f32[32,8]{0,1:T(8,128)S(1)}, f32[32,8]{0,1:T(8,128)}, u32[]{:S(2)}) copy-start(f32[32,8]{0,1:T(8,128)} %param.15) | copy-start | bytes 3076
  6.6 22.7 %copy-start.9 = (s32[1,1,2,16]{3,2,1,0:T(2,128)S(1)}, s32[1,1,2,16]{3,2,1,0:T(2,128)}, u32[]{:S(2)}) copy-start(s32[1,1,2,16]{3,2,1,0:T(2,128)} %param.17) | copy-start | bytes 388
  6.6 22.7 %copy-start.10 = (f32[8]{0:T(128)S(1)}, f32[8]{0:T(128)}, u32[]{:S(2)}) copy-start(f32[8]{0:T(128)} %slope.1) | copy-start | bytes 100
  35.4 38.6 %copy-start.5 = (bf16[128,1024]{1,0:T(8,128)(2,1)S(1)}, bf16[128,1024]{1,0:T(8,128)(2,1)}, u32[]{:S(2)}) copy-start(bf16[128,1024]{1,0:T(8,128)(2,1)} %x_in.1) | copy-start | bytes 786436
where the time goes:
time: 74.6 us; the launch traced here: 75.3 us
  Pallas kernels  67.4 us (90%)
  local copies, waits for them, and re-layouts  6.63 us (9%)
  matrix products  1.18 us (2%)
    pallas_call x1, Pallas kernels, local(): pl.pallas_call(functools.partial(combine, n_chip), out_shape=jax.ShapeDty...  38.6 us
    pallas_call x1, Pallas kernels, local(): pl.pallas_call(functools.partial(exchange, n_row, n_chip), out_shape=(jax...  22.6 us
    unnamed x22, local copies, waits for them, and re-layouts  6.63 us
    pallas_call x1, Pallas kernels, local(): pl.pallas_call(functools.partial(attend, slot_cap, dim ** (-0.5)), out_sh...  6.12 us

commit v1 on v0

v1 whole, which is shorter than its diff:
```python
import functools

import jax
import jax.numpy as jnp
from jax import lax
from jax.experimental import pallas as pl
from jax.experimental.pallas import tpu as pltpu
from jax.sharding import PartitionSpec as P

EPSILON = 1e-05
LOW_FLOOR = -1e30
CORES = 2
MESH = pl.DeviceIdType.MESH
LANES = 128
CHUNK_HEADS = 2
TAIL = 16
EARLY_BYTES = 12 * 2**20
VMEM_BYTES = 67043328


def normalize(features, gain_vec):
    as_float = features.astype(jnp.float32)
    centered = as_float - jnp.mean(as_float, axis=-1, keepdims=True)
    variance = jnp.mean(centered * centered, axis=-1, keepdims=True)
    return (centered * lax.rsqrt(variance + EPSILON) * gain_vec).astype(jnp.bfloat16)


def target_of(index, k, n):
    if n & (n - 1):
        return (index + k) % n
    return index ^ k


def source_of(index, k, n):
    if n & (n - 1):
        return (index + n - k) % n
    return index ^ k


def pick(index, values):
    if all(v == values[0] for v in values):
        return values[0]
    out = values[0]
    for at, value in enumerate(values[1:], 1):
        out = jnp.where(index == at, value, out)
    return out


def proxied(source, dest, n):
    return (source == 0 and dest >= 2) or (source == n - 1 and dest <= n - 3)


def route_tables(n):
    now, later, incoming = [], [], []
    for z in range(n):
        others = sorted((d for d in range(n) if d != z), key=lambda d: -abs(d - z))
        relay = {d for d in others if (z == 1 and proxied(0, d, n)) or (z == n - 2 and proxied(n - 1, d, n))}
        now.append([d for d in others if d not in relay])
        later.append([d for d in others if d in relay])
        incoming.append([s for s in others[::-1] if not proxied(s, z, n)])
    return now, later, incoming


def padded(rows, fill):
    longest = max(map(len, rows))
    return [[row[j] if j < len(row) else fill(z) for z, row in enumerate(rows)] for j in range(longest)]


def split_level(level):
    high = level.astype(jnp.bfloat16).astype(jnp.float32)
    rest = level - high
    middle = rest.astype(jnp.bfloat16).astype(jnp.float32)
    low = rest - middle
    filler = jnp.zeros((TAIL - 3 * level.shape[0], level.shape[1]), jnp.float32)
    return jnp.concatenate([high, middle, low, filler], axis=0).astype(jnp.bfloat16)


def join_level(tail, count):
    tail = tail.astype(jnp.float32)
    return tail[:count] + tail[count : 2 * count] + tail[2 * count : 3 * count]


def layer(
    n_row, n_chip, early, scale, pairs, slope, x_in, gain_in, wq_in, wkv_in, wo_in, table_in, b_in, e_in, out_ref, *scratch
):
    scratch = list(scratch)
    chunks = x_in.shape[1] // (CHUNK_HEADS * (x_in.shape[1] // slope.shape[0]))
    q_all = [scratch.pop(0) for _ in range(chunks)]
    (
        x_buf, n_in, n_buf, wq_buf, wkv_buf, wo_buf, k_buf, v_buf, b_buf, e_all, bias, table,
        o_slot, m_slot, s_slot, codes, lookup, sib_out, sib_in, mix_out, via_in, got_in, own_o, own_l, acc,
        load_sem, x_sem, e_sem, q_send, q_recv, pair_send, pair_recv,
        sib_send, sib_recv, mix_send, via_recv, got_recv,
    ) = scratch
    row, col = lax.axis_index("row"), lax.axis_index("col")
    chip, core = col // CORES, col % CORES
    n_col = n_chip * CORES
    tile, width = x_in.shape
    heads = slope.shape[0]
    dim = width // heads
    hc = CHUNK_HEADS
    cw = hc * dim
    slot_cap = e_in.shape[1]
    slots = n_row * slot_cap
    f32, bf16 = jnp.float32, jnp.bfloat16
    sibling = (row, chip * CORES + (1 - core))
    chip_at = lambda z: (row, z * CORES + core)
    targets = [target_of(row, k, n_row) for k in range(1, n_row)]
    sources = [source_of(row, k, n_row) for k in range(1, n_row)]

    def load(src, dst, spot):
        copy = pltpu.make_async_copy(src, dst, load_sem.at[spot])
        copy.start()
        return copy

    def remote(src, dst, send, recv, where):
        return pltpu.make_async_remote_copy(
            src_ref=src, dst_ref=dst, send_sem=send, recv_sem=recv, device_id=where, device_id_type=MESH
        )

    x_load = load(x_in, x_buf, 0)
    wq_load = load(wq_in, wq_buf, 1)
    barrier = pltpu.get_barrier_semaphore()
    partners = [chip_at(target_of(chip, k, n_chip)) for k in range(1, n_chip)]
    if n_chip & (n_chip - 1):
        partners = [chip_at((chip + k) % n_chip) for k in range(1, n_chip)]
    partners = partners + [sibling] + [(r, col) for r in targets]
    for where in partners:
        pl.semaphore_signal(barrier, inc=1, device_id=where, device_id_type=MESH)
    b_load = load(b_in, b_buf, 2)
    own_e = load(e_in.at[row], e_all.at[row], 3)
    wkv_load = load(wkv_in, wkv_buf, 4)
    wo_load = load(wo_in, wo_buf, 5)

    table[...] = jnp.zeros(table.shape, f32)
    table[:, : table_in.shape[1]] = table_in[...]
    o_slot[slots] = jnp.zeros(o_slot.shape[1:], f32)
    m_slot[slots] = jnp.full(m_slot.shape[1:], LOW_FLOOR, f32)
    s_slot[slots] = jnp.zeros(s_slot.shape[1:], f32)

    x_load.wait()
    n_in[...] = normalize(x_buf[...], gain_in[...])
    pl.semaphore_wait(barrier, len(partners))

    x_copies = [
        remote(n_in, n_buf.at[k], x_sem.at[0, k], x_sem.at[1, k], (targets[k], col)) for k in range(n_row - 1)
    ]
    e_copies = [
        remote(e_in.at[targets[k]], e_all.at[row], e_sem.at[0, k], e_sem.at[1, k], (targets[k], col))
        for k in range(n_row - 1)
    ]
    for copy in x_copies + e_copies:
        copy.start()

    def e_arrival(k):
        there = e_all.at[sources[k]]
        return remote(there, there, e_sem.at[0, k], e_sem.at[1, k], (targets[k], col))

    def q_copy(c, k):
        here = q_all[c].at[col]
        return remote(here, here, q_send.at[c, k], q_recv.at[c, k], chip_at(target_of(chip, k + 1, n_chip)))

    def q_arrival(c, k):
        there = q_all[c].at[source_of(chip, k + 1, n_chip) * CORES + core]
        return remote(there, there, q_send.at[c, k], q_recv.at[c, k], sibling)

    def pair_copy(c, k, mine):
        origin = source_of(chip, k, n_chip) if k else chip
        there = q_all[c].at[origin * CORES + (core if mine else 1 - core)]
        return remote(there, there, pair_send.at[c, k], pair_recv.at[c, k], sibling)

    wq_load.wait()
    for c in range(chunks):
        cols = slice(c * cw, (c + 1) * cw)
        q_all[c][col] = jnp.dot(n_in[...], wq_buf[:, cols], preferred_element_type=f32).astype(bf16)
        for k in reversed(range(n_chip - 1)):
            q_copy(c, k).start()
        pair_copy(c, 0, True).start()

    @pl.loop(0, slots)
    def _(v):
        codes[v] = jnp.where(pairs[0, v] >= 0, pairs[0, v] * n_row + pairs[1, v] + v // slot_cap, -1)

    @pl.loop(0, n_col * n_row)
    def _(spot):
        found = jnp.int32(slots)
        for v in range(slots):
            found = jnp.where(codes[v] == spot, v, found)
        lookup[spot] = found

    def make_bias(owner, first, count):
        def one(k, carry):
            slot = owner * slot_cap + k
            buckets = b_buf[slot].T
            edges = e_all[owner, k].astype(f32).T
            for j in range(count):
                h = first + j
                entries = jnp.broadcast_to(table[h : h + 1, :], (tile, tile))
                picked = jnp.take_along_axis(entries, buckets, axis=1, mode="promise_in_bounds")
                bias[slot, j] = picked + slope[h] * edges
            return carry

        lax.fori_loop(0, slot_cap, one, 0)

    step = min(2 * LANES, width)

    def project(rows_ref, spot):
        hidden = rows_ref[...]

        @pl.loop(0, width // step)
        def _(at):
            left = pl.multiple_of(at * step, step)
            k_buf[spot, :, pl.ds(left, step)] = jnp.dot(
                hidden, wkv_buf[:, pl.ds(left, step)], preferred_element_type=f32
            ).astype(bf16)
            right = pl.multiple_of(width + left, step)
            value = jnp.dot(hidden, wkv_buf[:, pl.ds(right, step)], preferred_element_type=f32)
            v_buf[spot, pl.ds(left, step), :] = value.T.astype(bf16)

    def forward(c):
        for k in range(n_chip - 1):
            q_arrival(c, k).wait_recv()
            pair_copy(c, k + 1, True).start()

    b_load.wait()
    own_e.wait()
    if early:
        make_bias(row, 0, heads)
    wkv_load.wait()
    project(n_in, row)
    for k in range(n_row - 1):
        x_copies[k].wait_recv()
        project(n_buf.at[k], sources[k])
    forward(0)
    for k in range(n_row - 1):
        e_arrival(k).wait_recv()
        if early:
            make_bias(sources[k], 0, heads)

    group = slot_cap

    def attend(c):
        if not early:
            for r in range(n_row):
                make_bias(r, c * hc, hc)

        def one(t, carry):
            for k in range(group):
                v = t * group + k
                query = jnp.maximum(pairs[0, v], 0)
                key = pairs[1, v] + v // slot_cap
                tops, sums = [], []
                for j in range(hc):
                    h = c * hc + j
                    score = lax.dot_general(
                        k_buf[key, :, h * dim : (h + 1) * dim],
                        q_all[c][query, :, j * dim : (j + 1) * dim],
                        (((1,), (1,)), ((), ())),
                        preferred_element_type=f32,
                    )
                    score = score * scale + bias[v, h if early else j]
                    top = jnp.max(score, axis=0, keepdims=True)
                    probs = jnp.exp(score - top).astype(bf16)
                    tops.append(top)
                    sums.append(jnp.sum(probs.astype(f32), axis=0, keepdims=True))
                    o_slot[v, j * dim : (j + 1) * dim, :] = jnp.dot(
                        v_buf[key, h * dim : (h + 1) * dim, :], probs, preferred_element_type=f32
                    )
                m_slot[v] = jnp.concatenate(tops, axis=0)
                s_slot[v] = jnp.concatenate(sums, axis=0)
            return carry

        lax.fori_loop(0, slots // group, one, 0)

    def combine(levels, weights_of, parts):
        top = functools.reduce(jnp.maximum, levels)
        shares = [jnp.exp(level - top) for level in levels]
        total = functools.reduce(jnp.add, [s if w is None else s * w for s, w in zip(shares, weights_of)])
        live = total > 0.0
        safe = jnp.where(live, total, 1.0)
        level = jnp.where(live, top + jnp.log(safe), LOW_FLOOR)
        inverse = 1.0 / safe
        shares = [share * inverse for share in shares]
        out = []
        for j in range(hc):
            rows = slice(j * dim, (j + 1) * dim)
            out.append(
                functools.reduce(jnp.add, [s[j : j + 1] * part(rows).astype(f32) for s, part in zip(shares, parts)])
            )
        return out, level

    def reader(ref):
        return lambda rows: ref[rows, :]

    def merge(block, extras):
        levels, weights, parts = [], [], []
        for r in range(n_row):
            v = lookup[block * n_row + r]
            levels.append(m_slot[v])
            weights.append(s_slot[v])
            parts.append(functools.partial(lambda v, rows: o_slot[v, rows, :], v))
        for ref in extras:
            levels.append(join_level(ref[cw : cw + TAIL, :], hc))
            weights.append(None)
            parts.append(reader(ref))
        return combine(levels, weights, parts)

    def put(ref, out, level):
        for j in range(hc):
            ref[j * dim : (j + 1) * dim, :] = out[j].astype(bf16)
        ref[cw : cw + TAIL, :] = split_level(level)

    now, later, incoming = route_tables(n_chip)
    now_at = padded(now, lambda z: z)
    later_at = padded(later, lambda z: z) if any(later) else []
    from_at = padded(incoming, lambda z: z)

    def sib_copy(c, z, mine):
        return remote(sib_out.at[c, z], sib_in.at[c, z], sib_send.at[c, z], sib_recv.at[c, z], sibling)

    def far_order():
        return [pick(chip, [sorted(range(n_chip), key=lambda d: -abs(d - z))[j] for z in range(n_chip)]) for j in range(n_chip)]

    order = far_order()

    def to_sibling(c):
        for z in order:
            put(sib_out.at[c, z], *merge(z * CORES + (1 - core), []))
            sib_copy(c, z, True).start()

    def direct(c, z):
        return remote(mix_out.at[c, z], got_in.at[c, chip], mix_send.at[c, z], got_recv.at[c, chip], chip_at(z))

    def got_from(c, s):
        return remote(mix_out.at[c, s], got_in.at[c, s], mix_send.at[c, s], got_recv.at[c, s], chip_at(s))

    def to_proxy(c, z):
        where = pick(chip, [1 if at == 0 else n_chip - 2 for at in range(n_chip)])
        return remote(mix_out.at[c, z], via_in.at[c, z], mix_send.at[c, z], via_recv.at[c, z], chip_at(where))

    def flags(rows):
        return [[1 if j < len(row) else 0 for row in rows] for j in range(max(map(len, rows)))]

    now_flags, later_flags, from_flags = flags(now), flags(later), flags(incoming)

    def guard(values, run):
        if all(values):
            run()
        elif any(values):
            pl.when(pick(chip, values) == 1)(run)

    def send_now(c):
        for j, dests in enumerate(now_at):
            z = pick(chip, dests)
            passes = [int(f and proxied(at, d, n_chip)) for at, (f, d) in enumerate(zip(now_flags[j], dests))]
            straight = [int(f and not proxied(at, d, n_chip)) for at, (f, d) in enumerate(zip(now_flags[j], dests))]

            def run(z=z, passes=passes, straight=straight):
                sib_copy(c, z, False).wait_recv()
                put(mix_out.at[c, z], *merge(z * CORES + core, [sib_in.at[c, z]]))
                guard(passes, lambda: to_proxy(c, z).start())
                guard(straight, lambda: direct(c, z).start())

            guard(now_flags[j], run)
        sib_copy(c, chip, False).wait_recv()
        out, level = merge(chip * CORES + core, [sib_in.at[c, chip]])
        for j in range(hc):
            own_o[c, j * dim : (j + 1) * dim, :] = out[j]
        own_l[c] = level

    def send_later(c):
        for j, dests in enumerate(later_at):
            z = pick(chip, dests)

            def run(z=z):
                sib_copy(c, z, False).wait_recv()
                to_proxy(c, z).wait_recv()
                put(mix_out.at[c, z], *merge(z * CORES + core, [sib_in.at[c, z], via_in.at[c, z]]))
                direct(c, z).start()

            guard(later_flags[j], run)

    for j, origins in enumerate(from_at):
        if not all(from_flags[j]):
            s = pick(chip, origins)

            def blank(s=s):
                for c in range(chunks):
                    got_in[c, s, :cw, :] = jnp.zeros((cw, tile), bf16)
                    got_in[c, s, cw:, :] = split_level(jnp.full((hc, tile), LOW_FLOOR, f32))

            guard([1 - f for f in from_flags[j]], blank)

    def finish(c):
        levels, parts = [own_l[c]], [lambda rows: own_o[c, rows, :]]
        for j, origins in enumerate(from_at):
            s = pick(chip, origins)
            guard(from_flags[j], lambda: got_from(c, s).wait_recv())
            ref = got_in.at[c, s]
            levels.append(join_level(ref[cw : cw + TAIL, :], hc))
            parts.append(reader(ref))
        out, _ = combine(levels, [None] * len(levels), parts)
        attention = jnp.concatenate([o.astype(bf16) for o in out], axis=0)
        update = lax.dot_general(
            attention, wo_buf[c * cw : (c + 1) * cw, :], (((0,), (0,)), ((), ())), preferred_element_type=f32
        )
        if c == 0:
            acc[...] = x_buf[...].astype(f32) + update
        elif c < chunks - 1:
            acc[...] += update
        else:
            out_ref[...] = (acc[...] + update).astype(out_ref.dtype)

    wo_load.wait()
    for c in range(chunks):
        for k in range(n_chip):
            pair_copy(c, k, False).wait_recv()
        if c + 1 < chunks:
            forward(c + 1)
        attend(c)
        to_sibling(c)
        send_now(c)
        send_later(c)
        if c:
            finish(c - 1)
    finish(chunks - 1)

    for copy in x_copies + e_copies:
        copy.wait_send()
    for c in range(chunks):
        for k in range(n_chip - 1):
            q_copy(c, k).wait_send()
        for k in range(n_chip):
            pair_copy(c, k, True).wait_send()
            sib_copy(c, k, True).wait_send()
        for k in range(n_chip - 1):
            z = target_of(chip, k + 1, n_chip)
            direct(c, z).wait_send()


def local(
    n_row,
    n_col,
    node_features,
    norm_gain,
    w_query,
    w_keyvalue,
    w_out,
    bias_table,
    edge_slope,
    pair_blocks,
    bucket_ids,
    edge_weight,
):
    tile, width = node_features.shape
    heads = edge_slope.shape[0]
    dim = width // heads
    n_chip = n_col // CORES
    slot_cap = edge_weight.shape[3]
    slots = n_row * slot_cap
    hc = CHUNK_HEADS
    cw = hc * dim
    chunks = heads // hc
    bf16, f32 = jnp.bfloat16, jnp.float32
    vmem = pl.BlockSpec(memory_space=pltpu.VMEM)
    smem = pl.BlockSpec(memory_space=pltpu.SMEM)
    hbm = pl.BlockSpec(memory_space=pl.ANY)
    early = 4 * slots * heads * tile * tile <= EARLY_BYTES
    message = (chunks, n_chip, cw + TAIL, tile)
    dma = pltpu.SemaphoreType.DMA
    scratch = [pltpu.VMEM((n_col, tile, cw), bf16)] * chunks + [
        pltpu.VMEM((tile, width), bf16),
        pltpu.VMEM((tile, width), bf16),
        pltpu.VMEM((n_row - 1, tile, width), bf16),
        pltpu.VMEM(w_query.shape, bf16),
        pltpu.VMEM(w_keyvalue.shape, bf16),
        pltpu.VMEM(w_out.shape, bf16),
        pltpu.VMEM((n_row, tile, width), bf16),
        pltpu.VMEM((n_row, width, tile), bf16),
        pltpu.VMEM((slots, tile, tile), jnp.int32),
        pltpu.VMEM((n_row,) + edge_weight.shape[3:], bf16),
        pltpu.VMEM((slots, heads if early else hc, tile, tile), f32),
        pltpu.VMEM((heads, tile), f32),
        pltpu.VMEM((slots + 1, cw, tile), f32),
        pltpu.VMEM((slots + 1, hc, tile), f32),
        pltpu.VMEM((slots + 1, hc, tile), f32),
        pltpu.SMEM((slots,), jnp.int32),
        pltpu.SMEM((n_col * n_row,), jnp.int32),
        pltpu.VMEM(message, bf16),
        pltpu.VMEM(message, bf16),
        pltpu.VMEM(message, bf16),
        pltpu.VMEM(message, bf16),
        pltpu.VMEM(message, bf16),
        pltpu.VMEM((chunks, cw, tile), f32),
        pltpu.VMEM((chunks, hc, tile), f32),
        pltpu.VMEM((tile, width), f32),
        dma((6,)),
        dma((2, n_row - 1)),
        dma((2, n_row - 1)),
        dma((chunks, n_chip - 1)),
        dma((chunks, n_chip - 1)),
        dma((chunks, n_chip)),
        dma((chunks, n_chip)),
        dma((chunks, n_chip)),
        dma((chunks, n_chip)),
        dma((chunks, n_chip)),
        dma((chunks, n_chip)),
        dma((chunks, n_chip)),
    ]
    return pl.pallas_call(
        functools.partial(layer, n_row, n_chip, early, dim ** (-0.5)),
        out_shape=jax.ShapeDtypeStruct((tile, width), bf16),
        in_specs=[smem, smem, hbm, vmem, hbm, hbm, hbm, vmem, hbm, hbm],
        out_specs=vmem,
        scratch_shapes=scratch,
        compiler_params=pltpu.CompilerParams(collective_id=0, has_side_effects=True, vmem_limit_bytes=VMEM_BYTES),
        name="layer",
    )(
        pair_blocks.reshape(2, slots),
        edge_slope,
        node_features,
        norm_gain[None],
        w_query,
        w_keyvalue,
        w_out,
        bias_table.T,
        bucket_ids.reshape(slots, tile, tile),
        edge_weight[0, 0],
    )


def solution(mesh):
    return jax.shard_map(
        functools.partial(local, mesh.shape["row"], mesh.shape["col"]),
        mesh=mesh,
        in_specs=(
            P(("row", "col"), None),
            P(),
            P(),
            P(),
            P(),
            P(),
            P(),
            P("row", "col", None, None),
            P("row", "col", None, None, None),
            P("row", "col", None, None, None, None),
        ),
        out_specs=P(("row", "col"), None),
        check_vma=False,
    )
```

time: 74.6 us -> 76.8 us (1.029)
  the two profiles are of different devices: /device:TPU:11 before, /device:TPU:0 now
where the time goes in v1:
time: 76.8 us; the launch traced here: 76.6 us
  Pallas kernels  75 us (98%)
  local copies, waits for them, and re-layouts  1.67 us (2%)
    pallas_call x1, Pallas kernels, local(): pl.pallas_call(functools.partial(layer, n_row, n_chip, early, dim ** (-0....  75 us
    unnamed x1, local copies, waits for them, and re-layouts  1.67 us

profile of v1, /device:TPU:0, one launch (start us, length us, event | category | flops | bytes accessed | tf_op | source)
XLA Modules:
  0.0 76.6 jit_solution(1189226911989835153)
XLA Ops:
  0.0 75.0 %layer.1 = bf16[128,1024]{1,0:T(8,128)(2,1)} custom-call(s32[2,16]{1,0:T(2,128)} %bitcast.9, f32[8]{0:T(128)} %slope.1, bf16[128,1024]{1,0:T(8,128)(2,1)} %x_in.1, f32[1,1024]{1,0:T(1,128)} %bitcast.7, bf16[1024,1024]{1,0:T(8,128)(2,1)} %wq_in.1, bf16[1024,2048]{1,0:T(8,128)(2,1)} %wkv_in.1, bf16[1024,1024]{1,0:T(8,128)(2,1)} %wo_in.1, f32[8,32]{1,0:T(8,128)} %bitcast.8, ...), custom_call_target="tpu_custom_call" | custom-call | tf_op jit(solution)/shard_map/layer/pallas_call | solution.py:510
  75.0 1.7 %copy.12 = bf16[128,1024]{1,0:T(8,128)(2,1)} copy(bf16[128,1024]{1,0:T(8,128)(2,1)} %layer.1) | data formatting | bytes 524288

commit v2 on v1

--- a/solution.py
+++ b/solution.py
@@ -88,7 +88,7 @@
     q_all = [scratch.pop(0) for _ in range(chunks)]
     (
         x_buf, n_in, n_buf, wq_buf, wkv_buf, wo_buf, k_buf, v_buf, b_buf, e_all, bias, table,
-        o_slot, m_slot, s_slot, codes, lookup, sib_out, sib_in, mix_out, via_in, got_in, own_o, own_l, acc,
+        scores, o_slot, m_slot, s_slot, codes, lookup, sib_out, sib_in, mix_out, via_in, got_in, own_o, own_l, acc,
         load_sem, x_sem, e_sem, q_send, q_recv, pair_send, pair_recv,
         sib_send, sib_recv, mix_send, via_recv, got_recv,
     ) = scratch
@@ -245,11 +245,11 @@
                 make_bias(r, c * hc, hc)
 
         def one(t, carry):
+            units = []
             for k in range(group):
                 v = t * group + k
                 query = jnp.maximum(pairs[0, v], 0)
                 key = pairs[1, v] + v // slot_cap
-                tops, sums = [], []
                 for j in range(hc):
                     h = c * hc + j
                     score = lax.dot_general(
@@ -259,15 +259,19 @@
                         preferred_element_type=f32,
                     )
                     score = score * scale + bias[v, h if early else j]
-                    top = jnp.max(score, axis=0, keepdims=True)
-                    probs = jnp.exp(score - top).astype(bf16)
-                    tops.append(top)
-                    sums.append(jnp.sum(probs.astype(f32), axis=0, keepdims=True))
-                    o_slot[v, j * dim : (j + 1) * dim, :] = jnp.dot(
-                        v_buf[key, h * dim : (h + 1) * dim, :], probs, preferred_element_type=f32
-                    )
-                m_slot[v] = jnp.concatenate(tops, axis=0)
-                s_slot[v] = jnp.concatenate(sums, axis=0)
+                    scores[k * hc + j] = score
+                    units.append((v, key, h, j, jnp.max(score, axis=0, keepdims=True)))
+            tops, sums = [], []
+            for at, (v, key, h, j, top) in enumerate(units):
+                probs = jnp.exp(scores[at] - top).astype(bf16)
+                tops.append(top)
+                sums.append(jnp.sum(probs.astype(f32), axis=0, keepdims=True))
+                o_slot[v, j * dim : (j + 1) * dim, :] = jnp.dot(
+                    v_buf[key, h * dim : (h + 1) * dim, :], probs, preferred_element_type=f32
+                )
+            for k in range(group):
+                m_slot[t * group + k] = jnp.concatenate(tops[k * hc : (k + 1) * hc], axis=0)
+                s_slot[t * group + k] = jnp.concatenate(sums[k * hc : (k + 1) * hc], axis=0)
             return carry
 
         lax.fori_loop(0, slots // group, one, 0)
@@ -481,6 +485,7 @@
         pltpu.VMEM((n_row,) + edge_weight.shape[3:], bf16),
         pltpu.VMEM((slots, heads if early else hc, tile, tile), f32),
         pltpu.VMEM((heads, tile), f32),
+        pltpu.VMEM((slot_cap * hc, tile, tile), f32),
         pltpu.VMEM((slots + 1, cw, tile), f32),
         pltpu.VMEM((slots + 1, hc, tile), f32),
         pltpu.VMEM((slots + 1, hc, tile), f32),

time: 76.8 us -> 60.1 us (0.78)
  Pallas kernels: 75 us -> 58.2 us
    pallas_call x1, Pallas kernels: 75 us -> 58.2 us  [local(): pl.pallas_call(functools.partial(layer, n_row, n_chip, early, dim ** (-0....]
where the time goes in v2:
time: 60.1 us; the launch traced here: 59.9 us
  Pallas kernels  58.2 us (97%)
  local copies, waits for them, and re-layouts  1.67 us (3%)
    pallas_call x1, Pallas kernels, local(): pl.pallas_call(functools.partial(layer, n_row, n_chip, early, dim ** (-0....  58.2 us
    unnamed x1, local copies, waits for them, and re-layouts  1.67 us

profile of v2, /device:TPU:0, one launch (start us, length us, event | category | flops | bytes accessed | tf_op | source)
XLA Modules:
  0.0 59.9 jit_solution(12585288249050609900)
XLA Ops:
  0.0 58.2 %layer.1 = bf16[128,1024]{1,0:T(8,128)(2,1)} custom-call(s32[2,16]{1,0:T(2,128)} %bitcast.9, f32[8]{0:T(128)} %slope.1, bf16[128,1024]{1,0:T(8,128)(2,1)} %x_in.1, f32[1,1024]{1,0:T(1,128)} %bitcast.7, bf16[1024,1024]{1,0:T(8,128)(2,1)} %wq_in.1, bf16[1024,2048]{1,0:T(8,128)(2,1)} %wkv_in.1, bf16[1024,1024]{1,0:T(8,128)(2,1)} %wo_in.1, f32[8,32]{1,0:T(8,128)} %bitcast.8, ...), custom_call_target="tpu_custom_call" | custom-call | tf_op jit(solution)/shard_map/layer/pallas_call | solution.py:515
  58.2 1.7 %copy.12 = bf16[128,1024]{1,0:T(8,128)(2,1)} copy(bf16[128,1024]{1,0:T(8,128)(2,1)} %layer.1) | data formatting | bytes 524288

commit v3 on v2

--- a/solution.py
+++ b/solution.py
@@ -13,9 +13,10 @@
 MESH = pl.DeviceIdType.MESH
 LANES = 128
 CHUNK_HEADS = 2
-TAIL = 16
+TAIL = 8
 EARLY_BYTES = 12 * 2**20
 VMEM_BYTES = 67043328
+SPARE = 0
 
 
 def normalize(features, gain_vec):
@@ -88,7 +89,7 @@
     q_all = [scratch.pop(0) for _ in range(chunks)]
     (
         x_buf, n_in, n_buf, wq_buf, wkv_buf, wo_buf, k_buf, v_buf, b_buf, e_all, bias, table,
-        scores, o_slot, m_slot, s_slot, codes, lookup, sib_out, sib_in, mix_out, via_in, got_in, own_o, own_l, acc,
+        scores, o_slot, m_slot, s_slot, codes, lookup, sib_out, sib_in, mix_out, via_in, got_in, own_o, own_l,
         load_sem, x_sem, e_sem, q_send, q_recv, pair_send, pair_recv,
         sib_send, sib_recv, mix_send, via_recv, got_recv,
     ) = scratch
@@ -138,44 +139,86 @@
     m_slot[slots] = jnp.full(m_slot.shape[1:], LOW_FLOOR, f32)
     s_slot[slots] = jnp.zeros(s_slot.shape[1:], f32)
 
+    relayed = n_row == 4
+    direct_rows = range(n_row - 1 - relayed)
+    half = width // 2
+    sides = [slice(0, half), slice(half, width)]
+
+    def e_copy(k):
+        return remote(e_in.at[targets[k]], e_all.at[row], e_sem.at[0, k], e_sem.at[1, k], (targets[k], col))
+
+    def e_arrival(k):
+        there = e_all.at[sources[k]]
+        return remote(there, there, e_sem.at[0, k], e_sem.at[1, k], (targets[k], col))
+
+    def x_copy(k):
+        return remote(n_in, n_buf.at[k], x_sem.at[0, k], x_sem.at[1, k], (targets[k], col))
+
+    def relay_copy(side):
+        part = n_buf.at[1 - side, :, sides[side]]
+        there = n_buf.at[n_row - 2, :, sides[side]]
+        spot = n_row - 1 + side
+        return remote(part, there, x_sem.at[0, spot], x_sem.at[1, spot], (targets[side], col))
+
+    def line_copy(c, step, way):
+        there = q_all[c].at[(chip - way * step) * CORES + core]
+        origin = chip - way * step
+        return remote(there, there, q_send.at[c, step, (way + 1) // 2], q_recv.at[c, origin], chip_at(chip + way))
+
+    def line_arrival(c, step, way):
+        origin = chip - way * step
+        there = q_all[c].at[origin * CORES + core]
+        return remote(there, there, q_send.at[c, step, (way + 1) // 2], q_recv.at[c, origin], sibling)
+
+    def pair_copy(c, origin, mine):
+        there = q_all[c].at[origin * CORES + (core if mine else 1 - core)]
+        return remote(there, there, pair_send.at[c, origin], pair_recv.at[c, origin], sibling)
+
+    def inside(z):
+        return (z >= 0) & (z < n_chip)
+
+    def send_own(c):
+        for way in (1, -1):
+            pl.when(inside(chip + way))(lambda: line_copy(c, 0, way).start())
+        pair_copy(c, chip, True).start()
+
+    def wave(w):
+        for c in range(chunks):
+            step = w - c + 1
+            if not 1 <= step < n_chip:
+                continue
+            for way in (1, -1):
+                origin = chip - way * step
+
+                @pl.when(inside(origin))
+                def _():
+                    line_arrival(c, step, way).wait_recv()
+                    if step < n_chip - 1:
+                        pl.when(inside(chip + way))(lambda: line_copy(c, step, way).start())
+                    pair_copy(c, origin, True).start()
+
+        if w + 2 < chunks:
+            send_own(w + 2)
+
+    waves = list(range(chunks + n_chip - 2))
+
+    def next_wave():
+        if waves:
+            wave(waves.pop(0))
+
     x_load.wait()
     n_in[...] = normalize(x_buf[...], gain_in[...])
     pl.semaphore_wait(barrier, len(partners))
-
-    x_copies = [
-        remote(n_in, n_buf.at[k], x_sem.at[0, k], x_sem.at[1, k], (targets[k], col)) for k in range(n_row - 1)
-    ]
-    e_copies = [
-        remote(e_in.at[targets[k]], e_all.at[row], e_sem.at[0, k], e_sem.at[1, k], (targets[k], col))
-        for k in range(n_row - 1)
-    ]
-    for copy in x_copies + e_copies:
-        copy.start()
-
-    def e_arrival(k):
-        there = e_all.at[sources[k]]
-        return remote(there, there, e_sem.at[0, k], e_sem.at[1, k], (targets[k], col))
-
-    def q_copy(c, k):
-        here = q_all[c].at[col]
-        return remote(here, here, q_send.at[c, k], q_recv.at[c, k], chip_at(target_of(chip, k + 1, n_chip)))
-
-    def q_arrival(c, k):
-        there = q_all[c].at[source_of(chip, k + 1, n_chip) * CORES + core]
-        return remote(there, there, q_send.at[c, k], q_recv.at[c, k], sibling)
-
-    def pair_copy(c, k, mine):
-        origin = source_of(chip, k, n_chip) if k else chip
-        there = q_all[c].at[origin * CORES + (core if mine else 1 - core)]
-        return remote(there, there, pair_send.at[c, k], pair_recv.at[c, k], sibling)
-
+    for k in direct_rows:
+        x_copy(k).start()
+    for k in range(n_row - 1):
+        e_copy(k).start()
     wq_load.wait()
     for c in range(chunks):
         cols = slice(c * cw, (c + 1) * cw)
         q_all[c][col] = jnp.dot(n_in[...], wq_buf[:, cols], preferred_element_type=f32).astype(bf16)
-        for k in reversed(range(n_chip - 1)):
-            q_copy(c, k).start()
-        pair_copy(c, 0, True).start()
+        if c < 2:
+            send_own(c)
 
     @pl.loop(0, slots)
     def _(v):
@@ -188,16 +231,21 @@
             found = jnp.where(codes[v] == spot, v, found)
         lookup[spot] = found
 
-    def make_bias(owner, first, count):
+    def make_bias(owner, first, count, buckets_too=True, edges_too=True):
         def one(k, carry):
             slot = owner * slot_cap + k
-            buckets = b_buf[slot].T
-            edges = e_all[owner, k].astype(f32).T
+            if buckets_too:
+                buckets = b_buf[slot].T
+            if edges_too:
+                edges = e_all[owner, k].astype(f32).T
             for j in range(count):
                 h = first + j
-                entries = jnp.broadcast_to(table[h : h + 1, :], (tile, tile))
-                picked = jnp.take_along_axis(entries, buckets, axis=1, mode="promise_in_bounds")
-                bias[slot, j] = picked + slope[h] * edges
+                if buckets_too:
+                    entries = jnp.broadcast_to(table[h : h + 1, :], (tile, tile))
+                    term = jnp.take_along_axis(entries, buckets, axis=1, mode="promise_in_bounds")
+                else:
+                    term = bias[slot, j]
+                bias[slot, j] = term + slope[h] * edges if edges_too else term
             return carry
 
         lax.fori_loop(0, slot_cap, one, 0)
@@ -217,25 +265,34 @@
             value = jnp.dot(hidden, wkv_buf[:, pl.ds(right, step)], preferred_element_type=f32)
             v_buf[spot, pl.ds(left, step), :] = value.T.astype(bf16)
 
-    def forward(c):
-        for k in range(n_chip - 1):
-            q_arrival(c, k).wait_recv()
-            pair_copy(c, k + 1, True).start()
-
+    ahead = min(2, n_row - 1)
     b_load.wait()
     own_e.wait()
+    wkv_load.wait()
+    project(n_in, row)
     if early:
         make_bias(row, 0, heads)
-    wkv_load.wait()
-    project(n_in, row)
-    for k in range(n_row - 1):
-        x_copies[k].wait_recv()
+    next_wave()
+    if early:
+        for k in range(ahead):
+            make_bias(sources[k], 0, heads, edges_too=False)
+    for k in direct_rows:
+        x_copy(k).wait_recv()
+        if relayed:
+            relay_copy(1 - k).start()
+    next_wave()
+    for k in direct_rows:
         project(n_buf.at[k], sources[k])
-    forward(0)
     for k in range(n_row - 1):
         e_arrival(k).wait_recv()
         if early:
-            make_bias(sources[k], 0, heads)
+            make_bias(sources[k], 0, heads, buckets_too=k >= ahead)
+        if k == 1 or k == n_row - 2:
+            next_wave()
+    if relayed:
+        for side in range(2):
+            relay_copy(side).wait_recv()
+        project(n_buf.at[n_row - 2], sources[n_row - 2])
 
     group = slot_cap
 
@@ -372,14 +429,25 @@
             own_o[c, j * dim : (j + 1) * dim, :] = out[j]
         own_l[c] = level
 
+    def hold(c):
+        for j, dests in enumerate(later_at):
+            z = pick(chip, dests)
+
+            def run(z=z):
+                sib_copy(c, z, False).wait_recv()
+                put(mix_out.at[c, z], *merge(z * CORES + core, [sib_in.at[c, z]]))
+
+            guard(later_flags[j], run)
+
     def send_later(c):
         for j, dests in enumerate(later_at):
             z = pick(chip, dests)
 
             def run(z=z):
-                sib_copy(c, z, False).wait_recv()
                 to_proxy(c, z).wait_recv()
-                put(mix_out.at[c, z], *merge(z * CORES + core, [sib_in.at[c, z], via_in.at[c, z]]))
+                refs = [mix_out.at[c, z], via_in.at[c, z]]
+                levels = [join_level(ref[cw : cw + TAIL, :], hc) for ref in refs]
+                put(mix_out.at[c, z], *combine(levels, [None] * 2, [reader(ref) for ref in refs]))
                 direct(c, z).start()
 
             guard(later_flags[j], run)
@@ -409,37 +477,45 @@
             attention, wo_buf[c * cw : (c + 1) * cw, :], (((0,), (0,)), ((), ())), preferred_element_type=f32
         )
         if c == 0:
-            acc[...] = x_buf[...].astype(f32) + update
-        elif c < chunks - 1:
-            acc[...] += update
+            out_ref[...] = update
         else:
-            out_ref[...] = (acc[...] + update).astype(out_ref.dtype)
+            out_ref[...] += update
 
     wo_load.wait()
     for c in range(chunks):
-        for k in range(n_chip):
-            pair_copy(c, k, False).wait_recv()
-        if c + 1 < chunks:
-            forward(c + 1)
+        while waves and waves[0] < c + n_chip - 1:
+            next_wave()
+        for z in range(n_chip):
+            pair_copy(c, z, False).wait_recv()
         attend(c)
+        next_wave()
         to_sibling(c)
         send_now(c)
-        send_later(c)
+        hold(c)
         if c:
-            finish(c - 1)
-    finish(chunks - 1)
-
-    for copy in x_copies + e_copies:
-        copy.wait_send()
+            send_later(c - 1)
+        if c > 1:
+            finish(c - 2)
+    send_later(chunks - 1)
+    for c in range(max(chunks - 2, 0), chunks):
+        finish(c)
+
+    for k in range(n_row - 1):
+        e_copy(k).wait_send()
+    for k in direct_rows:
+        x_copy(k).wait_send()
+    if relayed:
+        for side in range(2):
+            relay_copy(side).wait_send()
     for c in range(chunks):
+        for way in (1, -1):
+            for step in range(n_chip - 1):
+                pl.when(inside(chip + way) & inside(chip - way * step))(lambda: line_copy(c, step, way).wait_send())
+        for z in range(n_chip):
+            pair_copy(c, z, True).wait_send()
+            sib_copy(c, z, True).wait_send()
         for k in range(n_chip - 1):
-            q_copy(c, k).wait_send()
-        for k in range(n_chip):
-            pair_copy(c, k, True).wait_send()
-            sib_copy(c, k, True).wait_send()
-        for k in range(n_chip - 1):
-            z = target_of(chip, k + 1, n_chip)
-            direct(c, z).wait_send()
+            direct(c, target_of(chip, k + 1, n_chip)).wait_send()
 
 
 def local(
@@ -468,7 +544,7 @@
     bf16, f32 = jnp.bfloat16, jnp.float32
     vmem = pl.BlockSpec(memory_space=pltpu.VMEM)
     smem = pl.BlockSpec(memory_space=pltpu.SMEM)
-    hbm = pl.BlockSpec(memory_space=pl.ANY)
+    hbm = pl.BlockSpec(memory_space=pltpu.HBM)
     early = 4 * slots * heads * tile * tile <= EARLY_BYTES
     message = (chunks, n_chip, cw + TAIL, tile)
     dma = pltpu.SemaphoreType.DMA
@@ -498,12 +574,11 @@
         pltpu.VMEM(message, bf16),
         pltpu.VMEM((chunks, cw, tile), f32),
         pltpu.VMEM((chunks, hc, tile), f32),
-        pltpu.VMEM((tile, width), f32),
         dma((6,)),
+        dma((2, n_row + 1)),
         dma((2, n_row - 1)),
-        dma((2, n_row - 1)),
-        dma((chunks, n_chip - 1)),
-        dma((chunks, n_chip - 1)),
+        dma((chunks, n_chip - 1, 2)),
+        dma((chunks, n_chip)),
         dma((chunks, n_chip)),
         dma((chunks, n_chip)),
         dma((chunks, n_chip)),
@@ -512,13 +587,13 @@
         dma((chunks, n_chip)),
         dma((chunks, n_chip)),
     ]
-    return pl.pallas_call(
+    update = pl.pallas_call(
         functools.partial(layer, n_row, n_chip, early, dim ** (-0.5)),
-        out_shape=jax.ShapeDtypeStruct((tile, width), bf16),
+        out_shape=jax.ShapeDtypeStruct((tile, width), f32),
         in_specs=[smem, smem, hbm, vmem, hbm, hbm, hbm, vmem, hbm, hbm],
         out_specs=vmem,
         scratch_shapes=scratch,
-        compiler_params=pltpu.CompilerParams(collective_id=0, has_side_effects=True, vmem_limit_bytes=VMEM_BYTES),
+        compiler_params=pltpu.CompilerParams(collective_id=0, has_side_effects=True, vmem_limit_bytes=VMEM_BYTES - SPARE),
         name="layer",
     )(
         pair_blocks.reshape(2, slots),
@@ -532,6 +607,7 @@
         bucket_ids.reshape(slots, tile, tile),
         edge_weight[0, 0],
     )
+    return (node_features.astype(f32) + update).astype(bf16)
 
 
 def solution(mesh):

time: 60.1 us -> 53.5 us (0.89)
  Pallas kernels: 58.2 us -> 51.4 us
  other arithmetic: 0 us -> 1.87 us
  local copies, waits for them, and re-layouts: 1.67 us -> 0 us
    pallas_call x1, Pallas kernels: 58.2 us -> 51.4 us  [local(): pl.pallas_call(functools.partial(layer, n_row, n_chip, early, dim ** (-0....]
    convert_element_type x0 -> x1, other arithmetic: none -> 1.87 us  [local(): return (node_features.astype(f32) + update).astype(bf16)]
    unnamed x1 -> x0, local copies, waits for them, and re-layouts: 1.67 us -> none
where the time goes in v3:
time: 53.5 us; the launch traced here: 53.3 us
  Pallas kernels  51.4 us (96%)
  other arithmetic  1.87 us (3%)
    pallas_call x1, Pallas kernels, local(): pl.pallas_call(functools.partial(layer, n_row, n_chip, early, dim ** (-0....  51.4 us
    convert_element_type x1, other arithmetic, local(): return (node_features.astype(f32) + update).astype(bf16)  1.87 us

profile of v3, /device:TPU:0, one launch (start us, length us, event | category | flops | bytes accessed | tf_op | source)
XLA Modules:
  0.0 53.3 jit_solution(16173388270821090207)
XLA Ops:
  0.0 51.4 %layer.1 = f32[128,1024]{1,0:T(8,128)} custom-call(s32[2,16]{1,0:T(2,128)} %bitcast.9, f32[8]{0:T(128)} %slope.1, bf16[128,1024]{1,0:T(8,128)(2,1)} %x_in.1, f32[1,1024]{1,0:T(1,128)} %bitcast.7, bf16[1024,1024]{1,0:T(8,128)(2,1)} %wq_in.1, bf16[1024,2048]{1,0:T(8,128)(2,1)} %wkv_in.1, bf16[1024,1024]{1,0:T(8,128)(2,1)} %wo_in.1, f32[8,32]{1,0:T(8,128)} %bitcast.8, ...), custom_call_target="tpu_custom_call" | custom-call | tf_op jit(solution)/shard_map/layer/pallas_call | solution.py:590
  51.4 1.9 %add_convert_fusion = bf16[128,1024]{1,0:T(8,128)(2,1)} fusion(f32[128,1024]{1,0:T(8,128)} %layer.1, bf16[128,1024]{1,0:T(8,128)(2,1)} %x_in.1), kind=kLoop, calls=%fused_computation | loop fusion | flops 393216 | bytes 1048576 | tf_op jit(solution)/shard_map/convert_element_type | solution.py:610

commit v4 on v3

--- a/solution.py
+++ b/solution.py
@@ -211,7 +211,7 @@
     pl.semaphore_wait(barrier, len(partners))
     for k in direct_rows:
         x_copy(k).start()
-    for k in range(n_row - 1):
+    for k in direct_rows:
         e_copy(k).start()
     wq_load.wait()
     for c in range(chunks):
@@ -280,21 +280,31 @@
         x_copy(k).wait_recv()
         if relayed:
             relay_copy(1 - k).start()
+    if relayed:
+        e_copy(n_row - 2).start()
     next_wave()
     for k in direct_rows:
         project(n_buf.at[k], sources[k])
-    for k in range(n_row - 1):
+    for k in direct_rows:
         e_arrival(k).wait_recv()
         if early:
             make_bias(sources[k], 0, heads, buckets_too=k >= ahead)
-        if k == 1 or k == n_row - 2:
+        if k == 1:
             next_wave()
     if relayed:
+        if early:
+            make_bias(sources[n_row - 2], 0, heads, edges_too=False)
         for side in range(2):
             relay_copy(side).wait_recv()
         project(n_buf.at[n_row - 2], sources[n_row - 2])
-
-    group = slot_cap
+        next_wave()
+        e_arrival(n_row - 2).wait_recv()
+        if early:
+            make_bias(sources[n_row - 2], 0, heads, buckets_too=False)
+    else:
+        next_wave()
+
+    group = scores.shape[0] // hc
 
     def attend(c):
         if not early:
@@ -494,10 +504,8 @@
         hold(c)
         if c:
             send_later(c - 1)
-        if c > 1:
-            finish(c - 2)
     send_later(chunks - 1)
-    for c in range(max(chunks - 2, 0), chunks):
+    for c in range(chunks):
         finish(c)
 
     for k in range(n_row - 1):
@@ -561,7 +569,7 @@
         pltpu.VMEM((n_row,) + edge_weight.shape[3:], bf16),
         pltpu.VMEM((slots, heads if early else hc, tile, tile), f32),
         pltpu.VMEM((heads, tile), f32),
-        pltpu.VMEM((slot_cap * hc, tile, tile), f32),
+        pltpu.VMEM((slot_cap * max(2, hc), tile, tile), f32),
         pltpu.VMEM((slots + 1, cw, tile), f32),
         pltpu.VMEM((slots + 1, hc, tile), f32),
         pltpu.VMEM((slots + 1, hc, tile), f32),

time: 53.5 us -> 52.7 us (0.985)
  Pallas kernels: 51.4 us -> 50.6 us
    pallas_call x1, Pallas kernels: 51.4 us -> 50.6 us  [local(): pl.pallas_call(functools.partial(layer, n_row, n_chip, early, dim ** (-0....]
where the time goes in v4:
time: 52.7 us; the launch traced here: 52.5 us
  Pallas kernels  50.6 us (96%)
  other arithmetic  1.87 us (4%)
    pallas_call x1, Pallas kernels, local(): pl.pallas_call(functools.partial(layer, n_row, n_chip, early, dim ** (-0....  50.6 us
    convert_element_type x1, other arithmetic, local(): return (node_features.astype(f32) + update).astype(bf16)  1.87 us

profile of v4, /device:TPU:0, one launch (start us, length us, event | category | flops | bytes accessed | tf_op | source)
XLA Modules:
  0.0 52.5 jit_solution(14981872684842065276)
XLA Ops:
  0.0 50.6 %layer.1 = f32[128,1024]{1,0:T(8,128)} custom-call(s32[2,16]{1,0:T(2,128)} %bitcast.9, f32[8]{0:T(128)} %slope.1, bf16[128,1024]{1,0:T(8,128)(2,1)} %x_in.1, f32[1,1024]{1,0:T(1,128)} %bitcast.7, bf16[1024,1024]{1,0:T(8,128)(2,1)} %wq_in.1, bf16[1024,2048]{1,0:T(8,128)(2,1)} %wkv_in.1, bf16[1024,1024]{1,0:T(8,128)(2,1)} %wo_in.1, f32[8,32]{1,0:T(8,128)} %bitcast.8, ...), custom_call_target="tpu_custom_call" | custom-call | tf_op jit(solution)/shard_map/layer/pallas_call | solution.py:598
  50.6 1.9 %add_convert_fusion = bf16[128,1024]{1,0:T(8,128)(2,1)} fusion(f32[128,1024]{1,0:T(8,128)} %layer.1, bf16[128,1024]{1,0:T(8,128)(2,1)} %x_in.1), kind=kLoop, calls=%fused_computation | loop fusion | flops 393216 | bytes 1048576 | tf_op jit(solution)/shard_map/convert_element_type | solution.py:618
